TPU v7x, 256 devices: a whole 4x4x8 slice. The times are simulated.
256 devices in a mesh: row: 16 (over x, z_lo), col: 16 (over z_hi, y, core).
Axes of the slice: x: 4, y: 4, z: 8 (z_hi: 2, z_lo: 4; z = z_hi * 4 + z_lo), core: 2. Of those that a mesh axis runs over, the one named last changes fastest.
Arguments:
- acts: bfloat16 [2048, 5120], P('col', 'row'), may hold values from -60 to 60
- out_grads: bfloat16 [2048, 13824], P('row', 'col'), may hold values from -0.06187184 to 0.06187184
- momentum: float32 [5120, 13824], P('row', 'col'), may hold values from -200 to 200
- weight: float32 [5120, 13824], P('row', 'col'), may hold values from -0.078125 to 0.078125
Outputs:
- momentum_new: float32 [5120, 13824], P('row', 'col')
- update: bfloat16 [5120, 13824], P('row', 'col')
- weight_new: float32 [5120, 13824], P('row', 'col')
All inputs are finite; a program needn't handle non-finite values.
Results may differ from a plain program's by a relative error of at most 0.014.
Values may be sent and summed in bfloat16 or wider, within the bound.
A program may use at most 64 MiB of HBM per device.

v0:
```python
import math

import jax
import jax.numpy as jnp
from jax import lax
from jax.sharding import PartitionSpec as P

D = 5120


def body(acts, out_grads, momentum, weight):
    token_acts = lax.all_gather(acts, "col", axis=0, tiled=True)
    slab_rows = token_acts
    gradient = lax.dot_general(
        slab_rows,
        lax.all_gather(out_grads, "row", axis=0, tiled=True),
        (((0,), (0,)), ((), ())),
        preferred_element_type=jnp.float32,
    )
    momentum_new = 0.95 * momentum + gradient
    blended = gradient + 0.95 * momentum_new
    rounded = blended.astype(jnp.bfloat16)
    col_panel = lax.all_gather(rounded, "row", axis=0, tiled=True)
    slab_rows = col_panel
    gram_tile = lax.psum_scatter(
        lax.dot_general(
            slab_rows, rounded, (((1,), (1,)), ((), ())), preferred_element_type=jnp.float32
        ).astype(jnp.bfloat16),
        "col",
        scatter_dimension=0,
        tiled=True,
    )
    gram_cols = lax.all_gather(gram_tile, "col", axis=0, tiled=True)
    gram_rows = lax.all_gather(gram_tile, "row", axis=1, tiled=True)
    gram_square = jnp.dot(gram_rows, gram_cols, preferred_element_type=jnp.float32)
    total_sum = lax.psum(jnp.sum(gram_square * gram_square), ("row", "col"))
    schatten = jnp.sqrt(total_sum + 1e-06)
    square_root = jnp.sqrt(schatten)
    fourth_root = jnp.sqrt(square_root)
    poly_tile = (
        -4.775 * gram_tile.astype(jnp.float32) / square_root + 2.0315 * gram_square / schatten
    ).astype(jnp.bfloat16)
    poly_cols = lax.all_gather(poly_tile, "col", axis=0, tiled=True)
    product = lax.dot_general(
        poly_cols, col_panel, (((0,), (0,)), ((), ())), preferred_element_type=jnp.float32
    )
    orthogonal = (3.4445 * rounded.astype(jnp.float32) + product) / fourth_root
    factor = math.sqrt(D)
    update = (factor * orthogonal).astype(jnp.bfloat16)
    weight_new = 0.998 * weight - 0.02 * factor * orthogonal
    return (momentum_new, update, weight_new)


def solution(mesh):
    in_specs = (P("col", "row"), P("row", "col"), P("row", "col"), P("row", "col"))
    out_specs = (P("row", "col"), P("row", "col"), P("row", "col"))
    return jax.shard_map(body, mesh=mesh, in_specs=in_specs, out_specs=out_specs, check_vma=False)
```

profile of v0, /device:TPU:1, one launch (start us, length us, event | category | flops | bytes accessed | tf_op | source)
XLA Modules:
  0.0 829.8 jit_solution(14348969872725976175)
XLA Ops:
  7.2 0.0 all-gather.7.cloned.1.call-start
  7.2 0.7 all-gather.7.cloned.1.call-update
  7.9 0.0 all-gather.9.cloned.1.call-start
  7.9 0.7 all-gather.9.cloned.1.call-update
  8.6 0.0 all-gather.11.cloned.1.call-start
  8.7 63.7 %all-gather.7.cloned.1.call-done = bf16[2048,320]{0,1:T(8,128)(2,1)} async-done(((bf16[128,320]{0,1:T(8,128)(2,1)}), bf16[2048,320]{0,1:T(8,128)(2,1)}) %all-gather.7.cloned.1.call-update) | async-done | bytes 1310736 | tf_op jit(solution)/shard_map/all_gather | solution.py:12
  72.4 90.5 %all-gather.9.cloned.1.call-done = bf16[2048,864]{0,1:T(8,128)(2,1)} async-done(((bf16[128,864]{0,1:T(8,128)(2,1)}), bf16[2048,864]{0,1:T(8,128)(2,1)}) %all-gather.9.cloned.1.call-update) | async-done | bytes 3538960 | tf_op jit(solution)/shard_map/all_gather | solution.py:16
  162.9 5.5 add_convert_fusion
  168.4 0.0 all-gather.11.cloned.1.call-update
  168.4 0.0 reduce-scatter.2.cloned.1.call-start
  168.4 210.8 %all-gather.11.cloned.1.call-done = bf16[5120,864]{1,0:T(8,128)(2,1)} async-done(((bf16[320,864]{1,0:T(8,128)(2,1)}), bf16[5120,864]{1,0:T(8,128)(2,1)}) %all-gather.11.cloned.1.call-update) | async-done | bytes 8847376 | tf_op jit(solution)/shard_map/all_gather | solution.py:23
  379.3 9.3 %convolution_convert_fusion = bf16[5120,320]{1,0:T(8,128)(2,1)} fusion(bf16[5120,864]{1,0:T(8,128)(2,1)} %all-gather.11.cloned.1.call-done, bf16[320,864]{1,0:T(8,128)(2,1)} %get-tuple-element.3), kind=kOutput, calls=%fused_computation | convolution fusion | flops 2832793600 | bytes 12677120 | tf_op jit(solution)/shard_map/dot_general | solution.py:26
  388.5 0.0 reduce-scatter.2.cloned.1.call-update
  388.6 0.0 all-gather.15.cloned.1.call-start
  388.6 98.2 %reduce-scatter.2.cloned.1.call-done = bf16[320,320]{1,0:T(8,128)(2,1)} async-done(((bf16[5120,320]{1,0:T(8,128)(2,1)}), bf16[320,320]{1,0:T(8,128)(2,1)}) %reduce-scatter.2.cloned.1.call-update) | async-done | bytes 204816 | tf_op jit(solution)/shard_map/reduce_scatter | solution.py:25
  486.8 0.0 all-gather.15.cloned.1.call-update
  486.8 0.0 all-gather.13.cloned.1.call-start
  486.9 1.8 copy.7
  488.7 0.0 all-gather.13.cloned.1.call-update
  488.7 0.0 copy-start
  488.7 0.0 copy-start.1
  488.7 0.0 copy-start.2
  488.7 0.0 all-gather.17.cloned.1.call-start
  488.8 74.5 %all-gather.15.cloned.1.call-done = bf16[5120,320]{1,0:T(8,128)(2,1)} async-done(((bf16[320,320]{1,0:T(8,128)(2,1)}), bf16[5120,320]{1,0:T(8,128)(2,1)}) %all-gather.15.cloned.1.call-update) | async-done | bytes 3276816 | tf_op jit(solution)/shard_map/all_gather | solution.py:33
  563.2 93.3 %all-gather.13.cloned.1.call-done = bf16[320,5120]{0,1:T(8,128)(2,1)} async-done(((bf16[320,320]{0,1:T(8,128)(2,1)}), bf16[320,5120]{0,1:T(8,128)(2,1)}) %all-gather.13.cloned.1.call-update) | async-done | bytes 3276816 | tf_op jit(solution)/shard_map/all_gather | solution.py:34
  656.5 5.8 multiply_reduce_fusion
  662.3 77.1 %psum.7 = f32[]{:T(128)} all-reduce(f32[]{:T(128)} %get-tuple-element.7), channel_id=1, replica_groups=mesh['row'=16,'col'=16] {'row','col'}, use_global_device_ids=true, to_apply=%region_2.0 | all-reduce | flops 1 | bytes 8 | tf_op jit(solution)/shard_map/psum | solution.py:36
  740.2 0.0 copy-done
  740.2 0.8 add_convert_fusion.1
  741.0 0.0 all-gather.17.cloned.1.call-update
  741.1 72.2 %all-gather.17.cloned.1.call-done = bf16[5120,320]{1,0:T(8,128)(2,1)} async-done(((bf16[320,320]{1,0:T(8,128)(2,1)}), bf16[5120,320]{1,0:T(8,128)(2,1)}) %all-gather.17.cloned.1.call-update) | async-done | bytes 3276816 | tf_op jit(solution)/shard_map/all_gather | solution.py:43
  813.3 0.0 copy-done.1
  813.3 0.0 copy-done.2
  813.3 9.7 %multiply_subtract_fusion = (f32[320,864]{1,0:T(8,128)}, bf16[320,864]{1,0:T(8,128)(2,1)}) fusion(f32[320,864]{1,0:T(8,128)S(1)} %copy-done.2, f32[]{:T(128)S(6)} %sqrt.11, bf16[5120,320]{1,0:T(8,128)(2,1)} %all-gather.17.cloned.1.call-done, bf16[5120,864]{1,0:T(8,128)(2,1)} %all-gather.11.cloned.1.call-done, bf16[320,864]{1,0:T(8,128)(2,1)S(1)} %copy-done.1), kind=kOutput, calls=%fused_computation.3 | convolution fusion | flops 2833643520 | bytes 15441924 | tf_op jit(solution)/shard_map/dot_general | solution.py:44
Async XLA Ops:
  7.2 65.2 %all-gather.7.cloned.1.call-start = ((), (), s32[]{:S(2)}) async-start(), calls=%async_computation.1 | async-start | bytes 1392640 | tf_op jit(solution)/shard_map/all_gather | solution.py:12
  7.9 155.0 %all-gather.9.cloned.1.call-start = ((), (), s32[]{:S(2)}) async-start(), calls=%async_computation.2 | async-start | bytes 3760128 | tf_op jit(solution)/shard_map/all_gather | solution.py:16
  8.6 370.6 %all-gather.11.cloned.1.call-start = ((), (), s32[]{:S(2)}) async-start(), calls=%async_computation.3 | async-start | bytes 9748480 | tf_op jit(solution)/shard_map/all_gather | solution.py:23
  168.4 318.4 %reduce-scatter.2.cloned.1.call-start = ((), (), s32[]{:S(2)}) async-start(), calls=%async_computation.4 | async-start | bytes 4177920 | tf_op jit(solution)/shard_map/reduce_scatter | solution.py:25
  388.6 174.7 %all-gather.15.cloned.1.call-start = ((), (), s32[]{:S(2)}) async-start(), calls=%async_computation.6 | async-start | bytes 4177920 | tf_op jit(solution)/shard_map/all_gather | solution.py:33
  486.8 169.7 %all-gather.13.cloned.1.call-start = ((), (), s32[]{:S(2)}) async-start(), calls=%async_computation.5 | async-start | bytes 4177920 | tf_op jit(solution)/shard_map/all_gather | solution.py:34
  488.7 251.5 %copy-start = (bf16[320,320]{1,0:T(8,128)(2,1)S(1)}, bf16[320,320]{1,0:T(8,128)(2,1)}, u32[]{:S(2)}) copy-start(bf16[320,320]{1,0:T(8,128)(2,1)} %reduce-scatter.2.cloned.1.call-done) | copy-start | bytes 614404
  488.7 324.6 %copy-start.1 = (bf16[320,864]{1,0:T(8,128)(2,1)S(1)}, bf16[320,864]{1,0:T(8,128)(2,1)}, u32[]{:S(2)}) copy-start(bf16[320,864]{1,0:T(8,128)(2,1)} %get-tuple-element.3) | copy-start | bytes 1658884
  488.7 324.6 %copy-start.2 = (f32[320,864]{1,0:T(8,128)S(1)}, f32[320,864]{1,0:T(8,128)}, u32[]{:S(2)}) copy-start(f32[320,864]{1,0:T(8,128)} %param.7) | copy-start | bytes 3317764
  488.7 324.5 %all-gather.17.cloned.1.call-start = ((), (), s32[]{:S(2)}) async-start(), calls=%async_computation.7 | async-start | bytes 4177920 | tf_op jit(solution)/shard_map/all_gather | solution.py:43
Sparse Core Ops, SparseCore 0:
  10.5 61.8 all-gather.6
  74.1 88.7 all-gather.8
  168.5 210.7 all-gather.10
  388.7 98.0 reduce-scatter.1
  489.4 73.8 all-gather.14
  565.5 91.0 all-gather.12
  741.1 72.0 all-gather.16
where the time goes:
time: 830 us
  waiting for transfers between devices  705 us (85%)
  blocking collectives  77.1 us (9%)
  matrix products  30.3 us (4%)
  between operations  14.9 us (2%)
    all_gather x1, waiting for transfers between devices, body(): col_panel = lax.all_gather(rounded, 'row', axis=0, tiled=True)  211 us
    reduce_scatter x1, waiting for transfers between devices, body(): lax.psum_scatter(lax.dot_general(slab_rows, rounded, (((1,), (1,)), ((),...  98.2 us
    all_gather x1, waiting for transfers between devices, body(): gram_rows = lax.all_gather(gram_tile, 'row', axis=1, tiled=True)  93.3 us
    all_gather x1, waiting for transfers between devices, body(): lax.all_gather(out_grads, 'row', axis=0, tiled=True)  90.5 us
    psum x1, blocking collectives, body(): total_sum = lax.psum(jnp.sum(gram_square * gram_square), ('row', 'col'))  77.1 us
    all_gather x1, waiting for transfers between devices, body(): gram_cols = lax.all_gather(gram_tile, 'col', axis=0, tiled=True)  74.5 us
    all_gather x1, waiting for transfers between devices, body(): poly_cols = lax.all_gather(poly_tile, 'col', axis=0, tiled=True)  72.2 us
    all_gather x1, waiting for transfers between devices, body(): token_acts = lax.all_gather(acts, 'col', axis=0, tiled=True)  63.7 us
  transfers between devices with their start and end apart: 7, of which 7 were waited for; matrix products, arithmetic and copies ran while one was open for 0% of the time, Pallas kernels for 0%

commit v1 on v0

v1 whole, which is shorter than its diff:
```python
import math

import jax
import jax.numpy as jnp
from jax import lax
from jax.experimental import pallas as pl
from jax.experimental.pallas import tpu as pltpu
from jax.sharding import PartitionSpec as P

D = 5120
MESH = pl.DeviceIdType.MESH
F32 = jnp.float32
BF16 = jnp.bfloat16
N_SEM = 480


def dot_nn(a, b):
    return jnp.dot(a, b, preferred_element_type=F32)


def dot_nt(a, b):
    return lax.dot_general(a, b, (((1,), (1,)), ((), ())), preferred_element_type=F32)


class Comm:
    def __init__(self, sems):
        self.sems = sems
        self.used = 0
        self.pending = []
        self.r = lax.axis_index("row")
        self.c = lax.axis_index("col")
        r, c = self.r, self.c
        self.x, self.zl = r // 4, r % 4
        self.zh, self.y, self.co = c // 8, (c // 2) % 4, c % 2
        self.s = self.zl // 2
        self.zm = self.zl + self.s * (3 - 2 * self.zl)
        self.inner = self.zm == 1

    def sem(self, n=1):
        base = self.used
        self.used += n
        assert self.used <= N_SEM
        return base

    def row_dev(self, xo, zo):
        return (((self.x + xo + 4) % 4) * 4 + self.zl + zo * (1 - 2 * self.s), self.c)

    def y_dev(self, yo):
        return (self.r, self.zh * 8 + ((self.y + yo) % 4) * 2 + self.co)

    def zh_dev(self):
        return (self.r, (1 - self.zh) * 8 + self.y * 2 + self.co)

    def core_dev(self):
        return (self.r, self.zh * 8 + self.y * 2 + 1 - self.co)

    def zs(self, j):
        v = (self.zm, 1 - self.zm, 2, 3)[j]
        return v + self.s * (3 - 2 * v)

    def send(self, src, dst, ssem, rsem, to, cond=None):
        copy = pltpu.make_async_remote_copy(
            src_ref=src, dst_ref=dst, send_sem=self.sems.at[ssem], recv_sem=self.sems.at[rsem],
            device_id=to, device_id_type=MESH,
        )
        if cond is None:
            copy.start()
        else:
            pl.when(cond)(copy.start)
        self.pending.append((copy, cond))

    def recv(self, dst, rsem, cond=None):
        copy = pltpu.make_async_remote_copy(
            src_ref=dst, dst_ref=dst, send_sem=self.sems.at[rsem], recv_sem=self.sems.at[rsem],
            device_id=self.core_dev(), device_id_type=MESH,
        )
        if cond is None:
            copy.wait_recv()
        else:
            pl.when(cond)(copy.wait_recv)

    def drain(self):
        for copy, cond in self.pending:
            if cond is None:
                copy.wait_send()
            else:
                pl.when(cond)(copy.wait_send)
        self.pending = []


def row_gather(cm, view, half, own):
    rz, rp, rm, h0, h1 = (cm.sem(4) for _ in range(5))
    sz, sz2, sp, sm, t0, t1 = (cm.sem(4) for _ in range(6))

    def block(xo, j):
        return ((cm.x + xo + 4) % 4) * 4 + cm.zs(j)

    def out_x(j):
        k, zs = block(0, j), cm.zs(j)
        src = own if j == 0 else view(k)
        cm.send(src, view(k), sp + j, rp + zs, cm.row_dev(1, 0))
        cm.send(src, view(k), sm + j, rm + zs, cm.row_dev(-1, 0))

    def on_x(j):
        k, zs = block(-1, j), cm.zs(j)
        cm.recv(view(k), rp + zs)
        cm.send(half(k, 0), half(k, 0), t0 + j, h0 + zs, cm.row_dev(1, 0))
        k = block(1, j)
        cm.recv(view(k), rm + zs)
        cm.send(half(k, 1), half(k, 1), t1 + j, h1 + zs, cm.row_dev(-1, 0))

    k = block(0, 0)
    cm.send(own, view(k), sz, rz + cm.zl, cm.row_dev(0, 1))
    cm.send(own, view(k), sz2, rz + cm.zl, cm.row_dev(0, -1), cm.inner)
    out_x(0)
    yield (0, 0)
    for j in range(1, 4):
        k, zs = block(0, j), cm.zs(j)
        cm.recv(view(k), rz + zs)
        cm.send(view(k), view(k), sz + j, rz + zs, cm.row_dev(0, 1 if j == 1 else -1), cm.inner)
        out_x(j)
        yield (0, j)
        on_x(j - 1)
        yield (1, j - 1)
        yield (-1, j - 1)
    on_x(3)
    yield (1, 3)
    yield (-1, 3)
    for j in range(4):
        k, zs = block(2, j), cm.zs(j)
        cm.recv(half(k, 0), h0 + zs)
        cm.recv(half(k, 1), h1 + zs)
        yield (2, j)


def col_gather(cm, view, own):
    rzh, ry, rc = cm.sem(), cm.sem(6), cm.sem(8)
    szh, sy, sc = cm.sem(), cm.sem(6), cm.sem(8)

    def idx(zh, yo):
        return zh * 8 + ((cm.y + yo) % 4) * 2 + cm.co

    me = idx(cm.zh, 0)
    cm.send(own, view(me), szh, rzh, cm.zh_dev())
    for i, yo in enumerate((1, 3, 2)):
        cm.send(own, view(me), sy + i, ry + i, cm.y_dev(yo))
    cm.send(own, view(me), sc, rc, cm.core_dev())
    yield 0
    k = idx(1 - cm.zh, 0)
    cm.recv(view(k), rzh)
    for i, yo in enumerate((1, 3, 2)):
        cm.send(view(k), view(k), sy + 3 + i, ry + 3 + i, cm.y_dev(yo))
    cm.send(view(k), view(k), sc + 4, rc + 4, cm.core_dev())
    yield 1
    for zo in (0, 1):
        for i, yo in enumerate((1, 3, 2)):
            k = idx(cm.zh + zo * (1 - 2 * cm.zh), -yo + 4)
            cm.recv(view(k), ry + 3 * zo + i)
            cm.send(view(k), view(k), sc + 4 * zo + 1 + i, rc + 4 * zo + 1 + i, cm.core_dev())
        yield 2 + zo
    for zo in (0, 1):
        for i, yo in enumerate((0, 1, 3, 2)):
            k = idx(cm.zh + zo * (1 - 2 * cm.zh), -yo + 4) + 1 - 2 * cm.co
            cm.recv(view(k), rc + 4 * zo + i)
        yield 4 + zo


def kernel(acts_ref, og_ref, m_hbm, w_hbm, mnew_ref, upd_ref, wnew_ref,
           actb, ogb, rb, pb, rcb, csb, ryb, rzb, gb, hb, sb, acc1, acc2, gsq, mv, wv, ss1, ss2,
           sems, lsem):
    cm = Comm(sems)
    r, c = cm.r, cm.c
    tr, tc = mnew_ref.shape
    tt = og_ref.shape[0]

    load_m = pltpu.make_async_copy(m_hbm, mv, lsem.at[0])
    load_w = pltpu.make_async_copy(w_hbm, wv, lsem.at[1])
    load_m.start()
    load_w.start()

    barrier = pltpu.get_barrier_semaphore()
    for i in range(1, 16):
        pl.semaphore_signal(barrier, inc=1, device_id=((r + i) % 16, c), device_id_type=MESH)
        pl.semaphore_signal(barrier, inc=1, device_id=(r, (c + i) % 16), device_id_type=MESH)
    pl.semaphore_wait(barrier, 30)

    def og_view(k):
        return ogb.at[pl.ds(pl.multiple_of(k * tt, tt), tt)]

    def og_half(k, h):
        return ogb.at[pl.ds(pl.multiple_of(k * tt + h * (tt // 2), tt // 2), tt // 2)]

    def act_view(k):
        return actb.at[:, pl.ds(pl.multiple_of(k * tt, tt), tt)]

    gc = col_gather(cm, act_view, acts_ref)
    gr = row_gather(cm, og_view, og_half, og_ref)
    next(gr)
    next(gc)
    og_view(r)[...] = og_ref[...]
    act_view(c)[...] = acts_ref[...]
    for event in gr:
        if event in ((0, 1), (0, 2), (0, 3), (1, 3)):
            next(gc)
    for _ in gc:
        pass
    acc1[...] = jnp.zeros_like(acc1)

    @pl.loop(0, 2048 // 256)
    def _(t):
        at = pl.multiple_of(t * 256, 256)
        acc1[...] += dot_nn(actb[:, pl.ds(at, 256)], ogb[pl.ds(at, 256), :])

    load_m.wait()
    gradient = acc1[...]
    m_new = 0.95 * mv[...] + gradient
    mnew_ref[...] = m_new
    rb[r] = (gradient + 0.95 * m_new).astype(BF16)

    rc1, sc1 = cm.sem(8), cm.sem(8)
    rcy, scy = cm.sem(6), cm.sem(8)
    rzx, szx = cm.sem(), cm.sem()
    done = []

    def pair_of(xo, far):
        near_pair = cm.s
        return ((cm.x + xo + 4) % 4) * 2 + near_pair + far * (1 - 2 * near_pair)

    def core_send(n, p):
        cm.send(pb.at[2 * p + 1 - cm.co], rcb.at[p], sc1 + n, rc1 + p, cm.core_dev())

    def core_done(n, p):
        cm.recv(rcb.at[p], rc1 + p)
        csb[p] = (pb[2 * p + cm.co].astype(F32) + rcb[p].astype(F32)).astype(BF16)
        zh, y = p // 4, p % 4
        slot = (cm.y + 3 - y + 4) % 4
        far = y != cm.y
        cm.send(csb.at[p], ryb.at[zh * 3 + slot % 3], scy + n, rcy + zh * 3 + slot % 3,
                (r, cm.zh * 8 + y * 2 + cm.co), far)

    def gram_block(k):
        pb[k] = dot_nt(rb[r], rb[k]).astype(BF16)

    pairs = {}
    order = []
    for xo, j in row_gather(cm, lambda k: rb.at[k], lambda k, h: rb.at[k, pl.ds(h * (tr // 2), tr // 2)], rb.at[r]):
        gram_block(((cm.x + xo + 4) % 4) * 4 + cm.zs(j))
        key = (xo, j // 2)
        pairs[key] = pairs.get(key, 0) + 1
        if pairs[key] == 2:
            n = len(order)
            p = pair_of(*key)
            core_send(n, p)
            if order:
                core_done(n - 1, order[-1])
            order.append(p)
    core_done(7, order[-1])

    def y_sum(zh):
        for i in range(3):
            cm.recv(ryb.at[zh * 3 + i], rcy + zh * 3 + i)
        return (csb[zh * 4 + cm.y].astype(F32) + ryb[zh * 3].astype(F32)
                + ryb[zh * 3 + 1].astype(F32) + ryb[zh * 3 + 2].astype(F32))

    far_sum = rcb.at[0]
    far_sum[...] = y_sum(1 - cm.zh).astype(BF16)
    cm.send(far_sum, rzb, szx, rzx, cm.zh_dev())
    near_sum = y_sum(cm.zh)
    cm.recv(rzb, rzx)
    tile = (near_sum + rzb[...].astype(F32)).astype(BF16)
    gb[c] = tile
    hb[r] = tile

    gc = col_gather(cm, lambda k: gb.at[k], gb.at[c])
    gr = row_gather(cm, lambda k: hb.at[k], lambda k, h: hb.at[k, pl.ds(h * (tr // 2), tr // 2)], hb.at[r])
    next(gr)
    next(gc)
    for event in gr:
        if event in ((0, 1), (0, 2), (0, 3), (1, 3), (-1, 3)):
            next(gc)
    for _ in gc:
        pass
    gsq[...] = jnp.zeros_like(gsq)

    @pl.loop(0, 16)
    def _(k):
        gsq[...] += dot_nn(gb[k], hb[k])

    sb[c] = gsq[...].astype(BF16)

    gc = col_gather(cm, lambda k: sb.at[k], sb.at[c])
    next(gc)
    squares = jnp.sum(gsq[...] * gsq[...], axis=0, keepdims=True)
    ss1[r] = jnp.broadcast_to(jnp.sum(squares, axis=1, keepdims=True), ss1.shape[1:])
    r1, s1, r2, s2 = cm.sem(16), cm.sem(16), cm.sem(16), cm.sem(16)
    for i in range(1, 16):
        cm.send(ss1.at[r], ss1.at[r], s1 + i, r1 + i, ((r + i) % 16, c))
    acc1[...] = jnp.zeros_like(acc1)
    acc2[...] = jnp.zeros_like(acc2)

    def gram_times(lo, hi):
        @pl.loop(lo, hi)
        def _(k):
            acc1[...] += dot_nn(gb[k], rb[k])

    def square_times(zh, co):
        @pl.loop(0, 4)
        def _(y):
            k = zh * 8 + y * 2 + co
            acc2[...] += dot_nn(sb[k], rb[k])

    gram_times(0, 6)
    for i in range(1, 16):
        cm.recv(ss1.at[(r - i + 16) % 16], r1 + i)
    ss2[c] = jnp.sum(ss1[...], axis=0)
    for i in range(1, 16):
        cm.send(ss2.at[c], ss2.at[c], s2 + i, r2 + i, (r, (c + i) % 16))
    next(gc)
    gram_times(6, 11)
    next(gc)
    gram_times(11, 16)
    square_times(cm.zh, cm.co)
    next(gc)
    square_times(1 - cm.zh, cm.co)
    next(gc)
    square_times(cm.zh, 1 - cm.co)
    next(gc)
    square_times(1 - cm.zh, 1 - cm.co)
    for _ in gc:
        pass
    for i in range(1, 16):
        cm.recv(ss2.at[(c - i + 16) % 16], r2 + i)
    total = jnp.sum(ss2[...], axis=0)[0:1, 0:1]
    schatten = jnp.sqrt(total + 1e-06)
    square_root = jnp.sqrt(schatten)
    fourth_root = jnp.sqrt(square_root)
    load_w.wait()
    product = -4.775 * acc1[...] / square_root + 2.0315 * acc2[...] / schatten
    orthogonal = (3.4445 * rb[r].astype(F32) + product) / fourth_root
    factor = math.sqrt(D)
    upd_ref[...] = (factor * orthogonal).astype(BF16)
    wnew_ref[...] = 0.998 * wv[...] - 0.02 * factor * orthogonal
    cm.drain()


def body(acts, out_grads, momentum, weight):
    tr, tc = momentum.shape
    tt = out_grads.shape[0]
    vmem = pl.BlockSpec(memory_space=pltpu.VMEM)
    hbm = pl.BlockSpec(memory_space=pl.ANY)
    block = (tr, tr)
    return pl.pallas_call(
        kernel,
        name="muon_step",
        out_shape=(
            jax.ShapeDtypeStruct((tr, tc), F32),
            jax.ShapeDtypeStruct((tr, tc), BF16),
            jax.ShapeDtypeStruct((tr, tc), F32),
        ),
        in_specs=[vmem, vmem, hbm, hbm],
        out_specs=[vmem, vmem, vmem],
        scratch_shapes=[
            pltpu.VMEM((tr, 16 * tt), BF16),
            pltpu.VMEM((16 * tt, tc), BF16),
            pltpu.VMEM((16, tr, tc), BF16),
            pltpu.VMEM((16,) + block, BF16),
            pltpu.VMEM((8,) + block, BF16),
            pltpu.VMEM((8,) + block, BF16),
            pltpu.VMEM((6,) + block, BF16),
            pltpu.VMEM(block, BF16),
            pltpu.VMEM((16,) + block, BF16),
            pltpu.VMEM((16,) + block, BF16),
            pltpu.VMEM((16,) + block, BF16),
            pltpu.VMEM((tr, tc), F32),
            pltpu.VMEM((tr, tc), F32),
            pltpu.VMEM(block, F32),
            pltpu.VMEM((tr, tc), F32),
            pltpu.VMEM((tr, tc), F32),
            pltpu.VMEM((16, 8, 128), F32),
            pltpu.VMEM((16, 8, 128), F32),
            pltpu.SemaphoreType.DMA((N_SEM,)),
            pltpu.SemaphoreType.DMA((2,)),
        ],
        compiler_params=pltpu.CompilerParams(
            collective_id=0, has_side_effects=True, vmem_limit_bytes=67043328
        ),
    )(acts.T, out_grads, momentum, weight)


def solution(mesh):
    in_specs = (P("col", "row"), P("row", "col"), P("row", "col"), P("row", "col"))
    out_specs = (P("row", "col"), P("row", "col"), P("row", "col"))
    return jax.shard_map(body, mesh=mesh, in_specs=in_specs, out_specs=out_specs, check_vma=False)
```

time: 830 us -> 249 us (0.30)
  waiting for transfers between devices: 705 us -> 0 us
  Pallas kernels: 0 us -> 242 us
  blocking collectives: 77.1 us -> 0 us
  matrix products: 30.3 us -> 0 us
  between operations: 14.9 us -> 0.66 us
    all_gather x6 -> x0, waiting for transfers between devices: 605 us -> none  [the longest x1 211 us: body(): col_panel = lax.all_gather(rounded, 'row', axis=0, tiled=True)]
    pallas_call x0 -> x1, Pallas kernels: none -> 242 us  [body(): pl.pallas_call(kernel, name='muon_step', out_shape=(jax.ShapeDtypeStruct(...]
    reduce_scatter x1 -> x0, waiting for transfers between devices: 98.2 us -> none  [body(): lax.psum_scatter(lax.dot_general(slab_rows, rounded, (((1,), (1,)), ((),...]
    psum x1 -> x0, blocking collectives: 77.1 us -> none  [body(): total_sum = lax.psum(jnp.sum(gram_square * gram_square), ('row', 'col'))]
    dot_general x4 -> x0, matrix products: 30.3 us -> none  [the longest x1 9.73 us: body(): lax.dot_general(poly_cols, col_panel, (((0,), (0,)), ((), ())), preferred...]
  transfers between devices with their start and end apart: 7 -> 0, of which waited for: 7 -> 0; matrix products, arithmetic and copies ran while one was open for 0% -> 0% of each run, Pallas kernels for 0% -> 0%
where the time goes in v1:
time: 249 us; the launch traced here: 248 us
  Pallas kernels  242 us (97%)
  local copies, waits for them, and re-layouts  6.04 us (2%)
    pallas_call x1, Pallas kernels, body(): pl.pallas_call(kernel, name='muon_step', out_shape=(jax.ShapeDtypeStruct(...  242 us
    unnamed x8, local copies, waits for them, and re-layouts  6.04 us

profile of v1, /device:TPU:1, one launch (start us, length us, event | category | flops | bytes accessed | tf_op | source)
XLA Modules:
  0.0 248.4 jit_solution(4475914043533415767)
XLA Ops:
  0.6 1.8 copy.7.og_ref
  2.4 241.7 %muon_step.1 = (f32[320,864]{1,0:T(8,128)}, bf16[320,864]{1,0:T(8,128)(2,1)}, f32[320,864]{1,0:T(8,128)}) custom-call(bf16[320,128]{1,0:T(8,128)(2,1)} %bitcast.1, bf16[128,864]{1,0:T(8,128)(2,1)} %copy.7.og_ref, f32[320,864]{1,0:T(8,128)} %m_hbm.1, f32[320,864]{1,0:T(8,128)} %w_hbm.1), custom_call_target="tpu_custom_call" | custom-call | tf_op jit(solution)/shard_map/muon_step/pallas_call | solution.py:352
  244.1 0.0 copy-start.1
  244.1 0.0 copy-start
  244.1 2.5 copy.11
  246.5 0.0 copy-done.1
  246.5 0.8 copy.12
  247.4 0.0 copy-done
  247.4 1.0 copy.13
Async XLA Ops:
  244.1 2.5 copy-start.1
  244.1 3.3 %copy-start = (f32[320,864]{1,0:T(8,128)S(1)}, f32[320,864]{1,0:T(8,128)}, u32[]{:S(2)}) copy-start(f32[320,864]{1,0:T(8,128)} %get-tuple-element.8) | copy-start | bytes 3317764

commit v2 on v0

v2 whole, which is shorter than its diff:
```python
import math

import jax
import jax.numpy as jnp
from jax import lax
from jax.experimental import pallas as pl
from jax.experimental.pallas import tpu as pltpu
from jax.sharding import PartitionSpec as P

D = 5120
MESH = pl.DeviceIdType.MESH
F32 = jnp.float32
BF16 = jnp.bfloat16
N_SEM = 200
PAIR = 640
WIDE = (384, 256)


def dot_nn(a, b):
    return jnp.dot(a, b, preferred_element_type=F32)


def dot_nt(a, b):
    return lax.dot_general(a, b, (((1,), (1,)), ((), ())), preferred_element_type=F32)


def ds(start, size, unit):
    return pl.ds(pl.multiple_of(start, unit), size)


class Comm:
    def __init__(self, sems):
        self.sems = sems
        self.used = 0
        self.drains = []
        self.r = lax.axis_index("row")
        self.c = lax.axis_index("col")
        r, c = self.r, self.c
        self.x, self.zl = r // 4, r % 4
        self.zh, self.y, self.co = c // 8, (c // 2) % 4, c % 2
        self.q = c // 2
        self.s = self.zl // 2
        self.zm = self.zl + self.s * (3 - 2 * self.zl)
        self.inner = self.zm == 1

    def sem(self, n=1):
        base = self.used
        self.used += n
        assert self.used <= N_SEM
        return base

    def row_dev(self, xo, zo):
        return (((self.x + xo + 4) % 4) * 4 + self.zl + zo * (1 - 2 * self.s), self.c)

    def y_dev(self, yo):
        return (self.r, self.zh * 8 + ((self.y + yo) % 4) * 2 + self.co)

    def zh_dev(self):
        return (self.r, (1 - self.zh) * 8 + self.y * 2 + self.co)

    def core_dev(self):
        return (self.r, self.q * 2 + 1 - self.co)

    def zs(self, j):
        v = (self.zm, 1 - self.zm, 2, 3)[j]
        return v + self.s * (3 - 2 * v)

    def row_block(self, xo, j):
        return ((self.x + xo + 4) % 4) * 4 + self.zs(j)

    def row_pair(self, xo, far):
        return ((self.x + xo + 4) % 4) * 2 + self.s + far * (1 - 2 * self.s)

    def copy(self, src, dst, ssem, rsem, to):
        return pltpu.make_async_remote_copy(
            src_ref=src, dst_ref=dst, send_sem=self.sems.at[ssem], recv_sem=self.sems.at[rsem],
            device_id=to, device_id_type=MESH,
        )

    def send(self, ref, ssem, rsem, to):
        self.copy(ref, ref, ssem, rsem, to).start()

    def recv(self, ref, rsem):
        self.copy(ref, ref, rsem, rsem, self.core_dev()).wait_recv()

    def drain_later(self, ref, ssem, cond=None):
        self.drains.append((ref, ssem, cond))

    def drain(self):
        for ref, ssem, cond in self.drains:
            def wait():
                self.copy(ref, ref, ssem, ssem, self.core_dev()).wait_send()
            if cond is None:
                wait()
            else:
                pl.when(cond)(wait)

    def cores(self, split):
        return ((0, self.co == 0), (1, self.co == 1)) if split else ((self.co, None),)


def guarded(cond):
    return pl.when(cond) if cond is not None else lambda f: f()


def row_gather(cm, view, span, na, nb, split=False):
    az, ap, am, ah = (cm.sem(4) for _ in range(4))
    bp, bm, bh, bz = cm.sem(), cm.sem(), cm.sem(), cm.sem(16)
    s_all, s_in = cm.sem(), cm.sem()
    ha, hb = na // 2, nb // 2
    sel = ((1, 0), (-1, 0))
    xi = {0: 0, 1: 1, -1: 2, 2: 3}

    def a(k, co, lo=0, n=na):
        return view(k, lo, n, co)

    def b(k, co, lo=0, n=nb):
        return view(k, na + lo, n, co)

    def each(f):
        for co, cond in cm.cores(split):
            guarded(cond)(lambda: f(co))

    def inner(f):
        pl.when(cm.inner)(f)

    def a_out(j):
        k, zs = cm.row_block(0, j), cm.zs(j)

        def f(co):
            cm.send(a(k, co), s_all, ap + zs, cm.row_dev(1, 0))
            cm.send(a(k, co), s_all, am + zs, cm.row_dev(-1, 0))
        each(f)

    def a_chain(j):
        k, zs = cm.row_block(0, j), cm.zs(j)

        def f(co):
            cm.recv(a(k, co), az + zs)
            inner(lambda: cm.send(a(k, co), s_in, az + zs, cm.row_dev(0, 1 if j == 1 else -1)))
        each(f)
        a_out(j)

    def a_ring(j):
        zs = cm.zs(j)

        def f(co):
            k = cm.row_block(-1, j)
            cm.recv(a(k, co), ap + zs)
            cm.send(a(k, co, 0, ha), s_all, ah + zs, cm.row_dev(1, 0))
            k = cm.row_block(1, j)
            cm.recv(a(k, co), am + zs)
            cm.send(a(k, co, ha, ha), s_all, ah + zs, cm.row_dev(-1, 0))
        each(f)

    def a_last(j):
        each(lambda co: cm.recv(a(cm.row_block(2, j), co), ah + cm.zs(j)))

    def b_out(xo):
        k = cm.row_block(xo, 0)

        def f(co):
            cm.send(b(k, co), s_all, bz + 4 * xi[xo] + cm.zl, cm.row_dev(0, 1))
            inner(lambda: cm.send(b(k, co), s_in, bz + 4 * xi[xo] + cm.zl, cm.row_dev(0, -1)))
        each(f)

    def b_chain(xo, j):
        k, sem = cm.row_block(xo, j), bz + 4 * xi[xo] + cm.zs(j)

        def f(co):
            cm.recv(b(k, co), sem)
            inner(lambda: cm.send(b(k, co), s_in, sem, cm.row_dev(0, 1 if j == 1 else -1)))
        each(f)

    def start(co):
        k = cm.r
        cm.send(b(k, co), s_all, bp, cm.row_dev(1, 0))
        cm.send(b(k, co), s_all, bm, cm.row_dev(-1, 0))
        cm.send(a(k, co), s_all, az + cm.zl, cm.row_dev(0, 1))
        inner(lambda: cm.send(a(k, co), s_in, az + cm.zl, cm.row_dev(0, -1)))

    def b_ring(co):
        k = cm.row_block(-1, 0)
        cm.recv(b(k, co), bp)
        cm.send(b(k, co, 0, hb), s_all, bh, cm.row_dev(1, 0))
        k = cm.row_block(1, 0)
        cm.recv(b(k, co), bm)
        cm.send(b(k, co, hb, hb), s_all, bh, cm.row_dev(-1, 0))

    each(start)
    a_out(0)
    b_out(0)
    yield "start"
    each(b_ring)
    b_out(1)
    b_out(-1)
    a_chain(1)
    b_chain(0, 1)
    yield (0, 0)
    a_ring(0)
    each(lambda co: cm.recv(b(cm.row_block(2, 0), co), bh))
    b_out(2)
    a_chain(2)
    b_chain(1, 1)
    b_chain(-1, 1)
    b_chain(0, 2)
    a_ring(1)
    yield (1, 0)
    yield (-1, 0)
    a_chain(3)
    b_chain(2, 1)
    b_chain(0, 3)
    yield (0, 1)
    b_chain(1, 2)
    b_chain(-1, 2)
    a_ring(2)
    b_chain(2, 2)
    a_ring(3)
    b_chain(1, 3)
    b_chain(-1, 3)
    yield (1, 1)
    yield (-1, 1)
    a_last(0)
    a_last(1)
    yield (2, 0)
    b_chain(2, 3)
    a_last(2)
    a_last(3)
    yield (2, 1)
    for co, cond in cm.cores(split):
        cm.drain_later(span(13 * na + 7 * nb, co), s_all, cond)
        both = cm.inner if cond is None else jnp.logical_and(cm.inner, cond)
        cm.drain_later(span(4 * na + 16 * nb, co), s_in, both)


def col_gather(cm, view, span, rows, split=False):
    rz, rp, rm, rh, rc = cm.sem(), cm.sem(2), cm.sem(2), cm.sem(2), cm.sem(8)
    s_all, s_core = cm.sem(), cm.sem()
    half = rows // 2

    def chip(zo, yo):
        return (cm.zh + zo * (1 - 2 * cm.zh)) * 4 + (cm.y + yo + 4) % 4

    def each(f):
        for co, cond in cm.cores(split):
            guarded(cond)(lambda: f(co))

    def full(q, co):
        return view(q, co, 0, rows)

    def out(zo, co):
        q = chip(zo, 0)
        cm.send(full(q, co), s_all, rp + zo, cm.y_dev(1))
        cm.send(full(q, co), s_all, rm + zo, cm.y_dev(3))
        cm.send(full(q, co), s_core, rc + 4 * zo, cm.core_dev())

    def start(co):
        cm.send(full(cm.q, co), s_all, rz, cm.zh_dev())
        out(0, co)

    def ring(zo, co):
        q = chip(zo, -1)
        cm.recv(full(q, co), rp + zo)
        cm.send(view(q, co, 0, half), s_all, rh + zo, cm.y_dev(1))
        cm.send(full(q, co), s_core, rc + 4 * zo + 1, cm.core_dev())
        q = chip(zo, 1)
        cm.recv(full(q, co), rm + zo)
        cm.send(view(q, co, half, half), s_all, rh + zo, cm.y_dev(3))
        cm.send(full(q, co), s_core, rc + 4 * zo + 2, cm.core_dev())

    def last(zo, co):
        q = chip(zo, 2)
        cm.recv(full(q, co), rh + zo)
        cm.send(full(q, co), s_core, rc + 4 * zo + 3, cm.core_dev())

    def other_z(co):
        cm.recv(full(chip(1, 0), co), rz)
        out(1, co)

    def other_core(co):
        for zo in (0, 1):
            for i, yo in enumerate((0, -1, 1, 2)):
                cm.recv(full(chip(zo, yo), 1 - co), rc + 4 * zo + i)

    each(start)
    yield 0
    each(lambda co: ring(0, co))
    yield 1
    each(other_z)
    each(lambda co: last(0, co))
    yield 2
    each(lambda co: ring(1, co))
    yield 3
    each(lambda co: last(1, co))
    yield 4
    each(other_core)
    for co, cond in cm.cores(split):
        cm.drain_later(span(7, co), s_all, cond)
        cm.drain_later(span(8, co), s_core, cond)
    yield 5


def kernel(acts_ref, og_hbm, m_hbm, w_hbm, mnew_ref, upd_ref, wnew_ref,
           actb, ogb, rb, pb, rcb, csb, ryb, rzb, gb, hb, sb, acc1, acc2, gsq, mv, wv, ss1, ss2,
           sems, lsem):
    cm = Comm(sems)
    r, c, q = cm.r, cm.c, cm.q
    tr, tc = mnew_ref.shape
    tt = og_hbm.shape[0]

    load_o = pltpu.make_async_copy(og_hbm, ogb.at[ds(r * tt, tt, tt)], lsem.at[2])
    load_a = pltpu.make_async_copy(acts_ref, actb.at[:, ds(c * tt, tt, tt)], lsem.at[3])
    load_m = pltpu.make_async_copy(m_hbm, mv, lsem.at[0])
    load_w = pltpu.make_async_copy(w_hbm, wv, lsem.at[1])
    load_o.start()
    load_a.start()
    load_m.start()
    load_w.start()

    barrier = pltpu.get_barrier_semaphore()
    for i in range(1, 16):
        pl.semaphore_signal(barrier, inc=1, device_id=((r + i) % 16, c), device_id_type=MESH)
        pl.semaphore_signal(barrier, inc=1, device_id=(r, (c + i) % 16), device_id_type=MESH)
    load_o.wait()
    load_a.wait()
    pl.semaphore_wait(barrier, 30)

    gr = row_gather(
        cm, lambda k, lo, n, co: ogb.at[ds(k * tt + lo, n, 16)], lambda n, co: ogb.at[pl.ds(0, n)],
        tt * 3 // 4, tt // 4,
    )
    gc = col_gather(
        cm, lambda p, co, lo, n: actb.at[pl.ds(lo, n), ds((p * 2 + co) * tt, tt, tt)],
        lambda n, co: actb.at[:, pl.ds(0, n * tt)], tr,
    )
    next(gr)
    next(gc)
    for event in gr:
        if event in ((0, 0), (-1, 0), (0, 1), (-1, 1)):
            next(gc)
    for _ in gc:
        pass
    acc1[...] = jnp.zeros_like(acc1)

    @pl.loop(0, 2048 // 256)
    def _(t):
        acc1[...] += dot_nn(actb[:, ds(t * 256, 256, 256)], ogb[ds(t * 256, 256, 256), :])

    load_m.wait()
    gradient = acc1[...]
    m_new = 0.95 * mv[...] + gradient
    mnew_ref[...] = m_new
    rb[ds(r * tr, tr, tr), :] = (gradient + 0.95 * m_new).astype(BF16)

    rc1, sc1 = cm.sem(8), cm.sem()
    rcy, scy = cm.sem(2), cm.sem()
    rzx, szx = cm.sem(), cm.sem()

    def cols(ref, p, co):
        return ref.at[:, ds(p * PAIR + co * WIDE[0], WIDE[co], 128)]

    def wide(ref, co):
        return ref.at[:, pl.ds(0, WIDE[co])]

    def core_send(p):
        for co, cond in cm.cores(True):
            @pl.when(cond)
            def _():
                cm.copy(cols(pb, p, 1 - co), wide(rcb.at[p], 1 - co), sc1, rc1 + p, cm.core_dev()).start()

    def core_done(p):
        zh, y = p // 4, p % 4
        slot = (cm.y + 3 - y + 4) % 4
        for co, cond in cm.cores(True):
            @pl.when(cond)
            def _():
                cm.recv(wide(rcb.at[p], co), rc1 + p)
                mine = cols(pb, p, co)[...].astype(F32) + wide(rcb.at[p], co)[...].astype(F32)
                wide(csb.at[p], co)[...] = mine.astype(BF16)

                @pl.when(y != cm.y)
                def _():
                    cm.copy(wide(csb.at[p], co), wide(ryb.at[zh * 3 + slot % 3], co), scy, rcy + zh,
                            (r, cm.zh * 8 + y * 2 + cm.co)).start()

    def gram_pair(p):
        pb[:, ds(p * PAIR, PAIR, 128)] = dot_nt(
            rb[ds(r * tr, tr, tr), :], rb[ds(p * PAIR, PAIR, 128), :]
        ).astype(BF16)

    gr = row_gather(
        cm, lambda k, lo, n, co: rb.at[ds(k * tr + lo, n, 16)], lambda n, co: rb.at[pl.ds(0, n)],
        256, 64,
    )
    next(gr)
    last = None
    for event in gr:
        p = cm.row_pair(*event)
        gram_pair(p)
        core_send(p)
        if last is not None:
            core_done(last)
        last = p
    core_done(last)

    def y_sum(zh, co):
        for i in range(3):
            pass
        cm.recv(ryb.at[ds(zh * 3, 3, 1), :, pl.ds(0, WIDE[co])], rcy + zh)
        return (wide(csb.at[zh * 4 + cm.y], co)[...].astype(F32)
                + wide(ryb.at[zh * 3], co)[...].astype(F32)
                + wide(ryb.at[zh * 3 + 1], co)[...].astype(F32)
                + wide(ryb.at[zh * 3 + 2], co)[...].astype(F32))

    for co, cond in cm.cores(True):
        @pl.when(cond)
        def _():
            far_sum = wide(rcb.at[0], co)
            far_sum[...] = y_sum(1 - cm.zh, co).astype(BF16)
            cm.copy(far_sum, wide(rzb, co), szx, rzx, cm.zh_dev()).start()
            near_sum = y_sum(cm.zh, co)
            cm.recv(wide(rzb, co), rzx)
            tile = (near_sum + wide(rzb, co)[...].astype(F32)).astype(BF16)
            cols(gb, q, co)[...] = tile
            hb[ds(r * tr, tr, tr), pl.ds(0, WIDE[co])] = tile

    for co, cond in cm.cores(True):
        cm.drain_later(pb.at[:, pl.ds(0, 8 * WIDE[1 - co])], sc1, cond)
        cm.drain_later(pb.at[:, pl.ds(0, 6 * WIDE[co])], scy, cond)
        cm.drain_later(wide(rzb, co), szx, cond)

    def panel(ref):
        return (lambda p, co, lo, n: ref.at[pl.ds(lo, n), ds(p * PAIR + co * WIDE[0], WIDE[co], 128)],
                lambda n, co: ref.at[:, pl.ds(0, n * WIDE[co])], tr, True)

    gc = col_gather(cm, *panel(gb))
    gr = row_gather(
        cm, lambda k, lo, n, co: hb.at[ds(k * tr + lo, n, 16), pl.ds(0, WIDE[co])],
        lambda n, co: hb.at[pl.ds(0, n), pl.ds(0, WIDE[co])], 256, 64, True,
    )
    next(gr)
    next(gc)
    gsq[...] = jnp.zeros_like(gsq)

    def square(p):
        g = gb[:, ds(p * PAIR, PAIR, 128)]
        gsq[:, 0:256] += dot_nn(g, hb[ds(p * PAIR, PAIR, 128), 0:256])

        @pl.when(cm.co == 0)
        def _():
            gsq[:, 256:384] += dot_nn(g, hb[ds(p * PAIR, PAIR, 128), 256:384])

    for event in gr:
        if event in ((0, 0), (-1, 0), (0, 1)):
            next(gc)
        if event == (-1, 1):
            for _ in gc:
                pass

            @pl.loop(0, 6)
            def _(i):
                xo = i // 2 + i // 4
                square(((cm.x + xo) % 4) * 2 + i % 2)
        if event[0] == 2:
            square(cm.row_pair(*event))

    for co, cond in cm.cores(True):
        @pl.when(cond)
        def _():
            cols(sb, q, co)[...] = gsq[:, 0:WIDE[co]].astype(BF16)

    gc = col_gather(cm, *panel(sb))
    next(gc)
    squares = jnp.sum(gsq[...] * gsq[...], axis=0, keepdims=True)
    ss1[r] = jnp.broadcast_to(jnp.sum(squares, axis=1, keepdims=True), ss1.shape[1:])
    r1, s1, r2, s2 = cm.sem(), cm.sem(), cm.sem(), cm.sem()
    for i in range(1, 16):
        cm.send(ss1.at[r], s1, r1, ((r + i) % 16, c))
    acc1[...] = jnp.zeros_like(acc1)
    acc2[...] = jnp.zeros_like(acc2)

    def gram_times(lo, hi):
        @pl.loop(lo, hi)
        def _(p):
            acc1[...] += dot_nn(gb[:, ds(p * PAIR, PAIR, 128)], rb[ds(p * PAIR, PAIR, 128), :])

    def square_times():
        @pl.loop(0, 8)
        def _(p):
            acc2[...] += dot_nn(sb[:, ds(p * PAIR, PAIR, 128)], rb[ds(p * PAIR, PAIR, 128), :])

    gram_times(0, 3)
    cm.recv(ss1.at[pl.ds(0, 15)], r1)
    ss2[c] = jnp.sum(ss1[...], axis=0)
    for i in range(1, 16):
        cm.send(ss2.at[c], s2, r2, (r, (c + i) % 16))
    cm.drain_later(ss1.at[pl.ds(0, 15)], s1)
    cm.drain_later(ss2.at[pl.ds(0, 15)], s2)
    next(gc)
    gram_times(3, 5)
    next(gc)
    gram_times(5, 8)
    for _ in gc:
        pass
    square_times()
    cm.recv(ss2.at[pl.ds(0, 15)], r2)
    total = jnp.sum(ss2[...], axis=0)[0:1, 0:1]
    schatten = jnp.sqrt(total + 1e-06)
    square_root = jnp.sqrt(schatten)
    fourth_root = jnp.sqrt(square_root)
    load_w.wait()
    product = -4.775 * acc1[...] / square_root + 2.0315 * acc2[...] / schatten
    orthogonal = (3.4445 * rb[ds(r * tr, tr, tr), :].astype(F32) + product) / fourth_root
    factor = math.sqrt(D)
    upd_ref[...] = (factor * orthogonal).astype(BF16)
    wnew_ref[...] = 0.998 * wv[...] - 0.02 * factor * orthogonal
    cm.drain()


def body(acts, out_grads, momentum, weight):
    tr, tc = momentum.shape
    tt = out_grads.shape[0]
    vmem = pl.BlockSpec(memory_space=pltpu.VMEM)
    hbm = pl.BlockSpec(memory_space=pl.ANY)
    block = (tr, WIDE[0])
    return pl.pallas_call(
        kernel,
        name="muon_step",
        out_shape=(
            jax.ShapeDtypeStruct((tr, tc), F32),
            jax.ShapeDtypeStruct((tr, tc), BF16),
            jax.ShapeDtypeStruct((tr, tc), F32),
        ),
        in_specs=[hbm, hbm, hbm, hbm],
        out_specs=[vmem, vmem, vmem],
        scratch_shapes=[
            pltpu.VMEM((tr, 16 * tt), BF16),
            pltpu.VMEM((16 * tt, tc), BF16),
            pltpu.VMEM((16 * tr, tc), BF16),
            pltpu.VMEM((tr, 16 * tr), BF16),
            pltpu.VMEM((8,) + block, BF16),
            pltpu.VMEM((8,) + block, BF16),
            pltpu.VMEM((6,) + block, BF16),
            pltpu.VMEM(block, BF16),
            pltpu.VMEM((tr, 16 * tr), BF16),
            pltpu.VMEM((16 * tr, WIDE[0]), BF16),
            pltpu.VMEM((tr, 16 * tr), BF16),
            pltpu.VMEM((tr, tc), F32),
            pltpu.VMEM((tr, tc), F32),
            pltpu.VMEM(block, F32),
            pltpu.VMEM((tr, tc), F32),
            pltpu.VMEM((tr, tc), F32),
            pltpu.VMEM((16, 8, 128), F32),
            pltpu.VMEM((16, 8, 128), F32),
            pltpu.SemaphoreType.DMA((N_SEM,)),
            pltpu.SemaphoreType.DMA((4,)),
        ],
        compiler_params=pltpu.CompilerParams(
            collective_id=0, has_side_effects=True, vmem_limit_bytes=67043328
        ),
    )(acts.T, out_grads, momentum, weight)


def solution(mesh):
    in_specs = (P("col", "row"), P("row", "col"), P("row", "col"), P("row", "col"))
    out_specs = (P("row", "col"), P("row", "col"), P("row", "col"))
    return jax.shard_map(body, mesh=mesh, in_specs=in_specs, out_specs=out_specs, check_vma=False)
```

time: 830 us -> 212 us (0.26)
  waiting for transfers between devices: 705 us -> 0 us
  Pallas kernels: 0 us -> 204 us
  blocking collectives: 77.1 us -> 0 us
  matrix products: 30.3 us -> 0 us
  between operations: 14.9 us -> 0.66 us
    all_gather x6 -> x0, waiting for transfers between devices: 605 us -> none  [the longest x1 211 us: body(): col_panel = lax.all_gather(rounded, 'row', axis=0, tiled=True)]
    pallas_call x0 -> x1, Pallas kernels: none -> 204 us  [body(): pl.pallas_call(kernel, name='muon_step', out_shape=(jax.ShapeDtypeStruct(...]
    reduce_scatter x1 -> x0, waiting for transfers between devices: 98.2 us -> none  [body(): lax.psum_scatter(lax.dot_general(slab_rows, rounded, (((1,), (1,)), ((),...]
    psum x1 -> x0, blocking collectives: 77.1 us -> none  [body(): total_sum = lax.psum(jnp.sum(gram_square * gram_square), ('row', 'col'))]
    dot_general x4 -> x0, matrix products: 30.3 us -> none  [the longest x1 9.73 us: body(): lax.dot_general(poly_cols, col_panel, (((0,), (0,)), ((), ())), preferred...]
  transfers between devices with their start and end apart: 7 -> 0, of which waited for: 7 -> 0; matrix products, arithmetic and copies ran while one was open for 0% -> 0% of each run, Pallas kernels for 0% -> 0%
where the time goes in v2:
time: 212 us; the launch traced here: 210 us
  Pallas kernels  204 us (96%)
  local copies, waits for them, and re-layouts  6.04 us (3%)
    pallas_call x1, Pallas kernels, body(): pl.pallas_call(kernel, name='muon_step', out_shape=(jax.ShapeDtypeStruct(...  204 us
    unnamed x8, local copies, waits for them, and re-layouts  6.04 us

profile of v2, /device:TPU:1, one launch (start us, length us, event | category | flops | bytes accessed | tf_op | source)
XLA Modules:
  0.0 210.3 jit_solution(16933138154635815836)
XLA Ops:
  0.6 1.8 copy.7.og_hbm
  2.4 203.6 %muon_step.1 = (f32[320,864]{1,0:T(8,128)}, bf16[320,864]{1,0:T(8,128)(2,1)}, f32[320,864]{1,0:T(8,128)}) custom-call(bf16[320,128]{1,0:T(8,128)(2,1)} %bitcast.1, bf16[128,864]{1,0:T(8,128)(2,1)} %copy.7.og_hbm, f32[320,864]{1,0:T(8,128)} %m_hbm.1, f32[320,864]{1,0:T(8,128)} %w_hbm.1), custom_call_target="tpu_custom_call" | custom-call | tf_op jit(solution)/shard_map/muon_step/pallas_call | solution.py:526
  206.0 0.0 copy-start.1
  206.0 0.0 copy-start
  206.1 2.5 %copy.11 = f32[320,864]{1,0:T(8,128)} copy(f32[320,864]{1,0:T(8,128)} %get-tuple-element.6) | data formatting | bytes 2211840
  208.5 0.0 copy-done.1
  208.5 0.8 copy.12
  209.3 0.0 copy-done
  209.3 1.0 copy.13
Async XLA Ops:
  206.0 2.5 %copy-start.1 = (bf16[320,864]{1,0:T(8,128)(2,1)S(1)}, bf16[320,864]{1,0:T(8,128)(2,1)}, u32[]{:S(2)}) copy-start(bf16[320,864]{1,0:T(8,128)(2,1)} %get-tuple-element.7) | copy-start | bytes 1658884
  206.0 3.3 %copy-start = (f32[320,864]{1,0:T(8,128)S(1)}, f32[320,864]{1,0:T(8,128)}, u32[]{:S(2)}) copy-start(f32[320,864]{1,0:T(8,128)} %get-tuple-element.8) | copy-start | bytes 3317764
